TPU v7x, 32 devices: a whole 2x2x4 slice. The times are simulated.
32 devices in a mesh: pair: 8 (over z, core), aux: 4 (over y, x).
Axes of the slice: x: 2, y: 2, z: 4, core: 2. Of those that a mesh axis runs over, the one named last changes fastest.
Arguments:
- factors: bfloat16 [384, 16, 64, 128], P('aux', 'pair'), may hold values from -1.75 to 1.75
- pairs: int32 [80, 2], replicated, may hold values from 0 to 15, as said below
- shared: int32 [80, 4], P(None, 'aux'), may hold values 0 or 1
- owners: int32 [80], replicated, may hold values from 0 to 7, as said below
Outputs:
- exchange_matrix: float32 [16, 128, 2048], P('pair', 'aux')
- pair_tiles: float32 [8, 40, 128, 128], P('pair', None, 'aux')
Inputs may be any that keep to these rules, and one draw needn't show every extreme that they name: Distinct pairs (a, b) with a <= b. `owners`: each device owns at most 40 pairs and one device owns exactly 40.
All inputs are finite; a program needn't handle non-finite values. No bound on the sum of `shared` on one device may be relied on, other than what follows from the above.
Results may differ from a plain program's by a relative error of at most 0.0003.
Values may be sent and summed in bfloat16 or wider, within the bound.
No kernel may reach another device: no remote copies, remote signals or barrier semaphores. Data moves between devices by JAX's collectives and lax.ppermute only.
A program may use at most 128 MiB of HBM per device.

v0:
```python
import jax
import jax.numpy as jnp
from jax import lax
from jax.sharding import PartitionSpec as P


def body(factors, pairs, shared, owners):
    aux_rows, tiles_here, orbitals, tile_width = factors.shape
    owner_count = lax.axis_size("pair")
    tile_count = tiles_here * owner_count
    basis_count = tile_count * tile_width
    pair_count = pairs.shape[0]
    shard_rows = tile_width // lax.axis_size("aux")
    myself = lax.axis_index("pair")
    column = lax.axis_index("aux")
    slot_count = 4 * (pair_count // owner_count)
    pair_ids = jnp.arange(pair_count, dtype=jnp.int32)
    same_owner = owners[:, None] == owners[None, :]
    owner_rank = jnp.sum(
        (same_owner & (pair_ids[None, :] < pair_ids[:, None])).astype(jnp.int32), axis=1
    )
    slot_ids = jnp.arange(slot_count, dtype=jnp.int32)
    matches = (owners[None, :] == myself) & (owner_rank[None, :] == slot_ids[:, None])
    picked = jnp.sum(jnp.where(matches, pair_ids[None, :], 0), axis=1)
    live_slot = jnp.any(matches, axis=1).astype(jnp.float32)
    left_ids = pairs[picked, 0]
    right_ids = pairs[picked, 1]
    weights = live_slot * shared[picked, 0].astype(jnp.float32)
    gathered = lax.all_gather(factors, "pair", axis=1, tiled=True)

    def contract(slot_item):
        left_id, right_id, slot_scale = slot_item
        left_block = lax.dynamic_index_in_dim(gathered, left_id, 1, keepdims=False).reshape(
            aux_rows * orbitals, tile_width
        )
        right_block = lax.dynamic_index_in_dim(gathered, right_id, 1, keepdims=False).reshape(
            aux_rows * orbitals, tile_width
        )
        product = lax.dot_general(
            left_block, right_block, (((0,), (0,)), ((), ())), preferred_element_type=jnp.float32
        )
        return product * slot_scale

    partial_tiles = lax.map(contract, (left_ids, right_ids, weights))
    summed = lax.psum(partial_tiles, "aux")
    direct = lax.dynamic_slice_in_dim(summed, column * shard_rows, shard_rows, 1)
    mirror = lax.dynamic_slice_in_dim(
        jnp.swapaxes(summed, 1, 2), column * shard_rows, shard_rows, 1
    )
    tile_ids = jnp.arange(tile_count, dtype=jnp.int32)
    off_diagonal = live_slot * (left_ids != right_ids).astype(jnp.float32)
    left_hot = (left_ids[:, None] == tile_ids[None, :]).astype(jnp.float32)
    right_hot = (right_ids[:, None] == tile_ids[None, :]).astype(jnp.float32)
    upper_part = jnp.einsum(
        "jt,jc,jrm->trcm",
        left_hot * live_slot[:, None],
        right_hot,
        direct,
        precision=lax.Precision.HIGHEST,
    )
    lower_part = jnp.einsum(
        "jt,jc,jrm->trcm",
        right_hot * off_diagonal[:, None],
        left_hot,
        mirror,
        precision=lax.Precision.HIGHEST,
    )
    contribution = (upper_part + lower_part).reshape(tile_count, shard_rows, basis_count)
    matrix_rows = lax.psum_scatter(contribution, "pair", scatter_dimension=0, tiled=True)
    owned_tiles = direct[None]
    return (matrix_rows, owned_tiles)


def solution(mesh):
    placed = (P("aux", "pair", None, None), P(), P(None, "aux"), P())
    return jax.shard_map(
        body,
        mesh=mesh,
        in_specs=placed,
        out_specs=(P("pair", "aux", None), P("pair", None, "aux", None)),
        check_vma=False,
    )
```

profile of v0, /device:TPU:0, one launch (start us, length us, event | category | flops | bytes accessed | tf_op | source)
XLA Modules:
  0.0 886.8 jit_solution(12804275647070934509)
XLA Ops:
  7.2 4.4 copy.20
  15.7 218.7 %all-gather.2.cloned.1.call-done = bf16[96,16,64,128]{3,2,0,1:T(8,128)(2,1)} async-done(((bf16[96,2,64,128]{3,2,0,1:T(8,128)(2,1)}), bf16[96,16,64,128]{3,2,0,1:T(8,128)(2,1)}) %all-gather.2.cloned.1.call-update) | async-done | bytes 25165840 | tf_op jit(solution)/shard_map/all_gather | solution.py:29
  234.4 26.9 %copy.21 = bf16[96,16,64,128]{3,0,2,1:T(8,128)(2,1)} copy(bf16[96,16,64,128]{3,2,0,1:T(8,128)(2,1)} %all-gather.2.cloned.1.call-done) | data formatting | bytes 50331648 | tf_op jit(solution)/shard_map/while | solution.py:44
  261.3 470.9 %while.10 = (s32[]{:T(128)}, f32[40,128,128]{2,0,1:T(8,128)}, s32[40]{0:T(128)S(1)}, bf16[96,16,64,128]{3,0,2,1:T(8,128)(2,1)}, s32[40]{0:T(128)S(1)}, /*index=5*/f32[40]{0:T(128)S(1)}, s32[]{:T(128)}, s32[]{:T(128)}, s32[]{:T(128)}) while((s32[]{:T(128)}, f32[40,128,128]{2,0,1:T(8,128)}, s32[40]{0:T(128)S(1)}, ...), condition=%wide.region_4.5_spmd, body=%wide.region_3.4_spmd.sunk | while | flops 201342976 | bytes 3343057 | solution.py:44
  361.0 3.2 fusion.42
  420.0 3.1 fusion.42
  431.8 3.2 fusion.42
  443.7 3.1 fusion.42
  490.7 3.1 fusion.42
  514.2 3.1 fusion.42
  526.0 3.2 fusion.42
  549.6 3.1 fusion.42
  573.1 3.1 fusion.42
  596.5 3.1 fusion.42
  620.0 3.1 fusion.42
  643.5 3.1 fusion.42
  655.3 3.1 fusion.42
  702.4 3.2 fusion.42
  732.5 76.4 %all-reduce.4.cloned.1.call-done = f32[40,128,128]{2,0,1:T(8,128)} async-done(((f32[40,128,128]{2,0,1:T(8,128)}), f32[40,128,128]{2,0,1:T(8,128)}) %all-reduce.4.cloned.1.call-update) | async-done | bytes 2621456 | tf_op jit(solution)/shard_map/psum | solution.py:45
  813.7 3.4 fusion.17
  817.2 3.6 add_bitcast_fusion
  820.8 4.4 copy.24
  825.1 4.9 reshape.48
  831.0 49.2 %reduce-scatter.2.cloned.1.call-done = f32[2,32,2048]{2,1,0:T(8,128)} async-done(((f32[16,32,2048]{2,1,0:T(8,128)}), f32[2,32,2048]{2,1,0:T(8,128)}) %reduce-scatter.2.cloned.1.call-update) | async-done | bytes 524304 | tf_op jit(solution)/shard_map/reduce_scatter | solution.py:69
  (219 shorter events, 281.1 us)
Async XLA Ops:
  7.2 5.4 copy-start
  7.2 227.2 %all-gather.2.cloned.1.call-start = ((), (), s32[]{:S(2)}) async-start(), calls=%async_computation.1 | async-start | bytes 28311552 | tf_op jit(solution)/shard_map/all_gather | solution.py:29
  11.6 0.7 copy-start.3
  11.6 3.1 copy-start.2
  11.6 797.3 %all-reduce.4.cloned.1.call-start = ((), (), s32[]{:S(2)}) async-start(), calls=%async_computation.2 | async-start | bytes 5242880 | tf_op jit(solution)/shard_map/psum | solution.py:45
  732.2 148.0 %reduce-scatter.2.cloned.1.call-start = ((), (), s32[]{:S(2)}) async-start(), calls=%async_computation.3 | async-start | bytes 4718592 | tf_op jit(solution)/shard_map/reduce_scatter | solution.py:69
  825.1 55.1 %copy-start.1 = (s32[80,2]{0,1:T(2,128)S(1)}, s32[80,2]{0,1:T(2,128)}, u32[]{:S(2)}) copy-start(s32[80,2]{0,1:T(2,128)} %param.7) | copy-start | bytes 1924
Sparse Core Ops, SparseCore 0:
  11.8 222.5 all-gather.1
  732.3 76.5 all-reduce.3
  830.2 49.9 reduce-scatter.1
where the time goes:
time: 891 us; the launch traced here: 887 us
  waiting for transfers between devices  344 us (39%)
  local copies, waits for them, and re-layouts  239 us (27%)
  loops' own time  156 us (18%)
  matrix products  133 us (15%)
  between operations  13.9 us (2%)
    all_gather x1, waiting for transfers between devices, body(): gathered = lax.all_gather(factors, 'pair', axis=1, tiled=True)  219 us
    another operation x1, loops' own time, body(): partial_tiles = lax.map(contract, (left_ids, right_ids, weights))  156 us
    dot_general x40, matrix products, contract(): lax.dot_general(left_block, right_block, (((0,), (0,)), ((), ())), prefer...  126 us
    dynamic_update_slice x40, local copies, waits for them, and re-layouts, body(): partial_tiles = lax.map(contract, (left_ids, right_ids, weights))  119 us
    psum x1, waiting for transfers between devices, body(): summed = lax.psum(partial_tiles, 'aux')  76.4 us
    dynamic_slice x120, local copies, waits for them, and re-layouts, body(): partial_tiles = lax.map(contract, (left_ids, right_ids, weights))  70.4 us
    reduce_scatter x1, waiting for transfers between devices, body(): lax.psum_scatter(contribution, 'pair', scatter_dimension=0, tiled=True)  49.2 us
    while x1, local copies, waits for them, and re-layouts, body(): partial_tiles = lax.map(contract, (left_ids, right_ids, weights))  26.9 us
  transfers between devices with their start and end apart: 3, of which 3 were waited for; matrix products, arithmetic and copies ran while one was open for 0% of the time, Pallas kernels for 0%

commit v1 on v0

--- a/solution.py
+++ b/solution.py
@@ -42,7 +42,7 @@
         return product * slot_scale
 
     partial_tiles = lax.map(contract, (left_ids, right_ids, weights))
-    summed = lax.psum(partial_tiles, "aux")
+    summed = jnp.sum(lax.all_gather(partial_tiles, "aux"), axis=0)
     direct = lax.dynamic_slice_in_dim(summed, column * shard_rows, shard_rows, 1)
     mirror = lax.dynamic_slice_in_dim(
         jnp.swapaxes(summed, 1, 2), column * shard_rows, shard_rows, 1

time: 891 us -> 830 us (0.932)
  local copies, waits for them, and re-layouts: 239 us -> 121 us
  waiting for transfers between devices: 344 us -> 371 us
  matrix products: 133 us -> 159 us
    dynamic_update_slice x40 -> x0, local copies, waits for them, and re-layouts: 119 us -> none  [body(): partial_tiles = lax.map(contract, (left_ids, right_ids, weights))]
    all_gather x0 -> x1, waiting for transfers between devices: none -> 103 us  [body(): summed = jnp.sum(lax.all_gather(partial_tiles, 'aux'), axis=0)]
    psum x1 -> x0, waiting for transfers between devices: 76.4 us -> none  [body(): summed = lax.psum(partial_tiles, 'aux')]
    dot_general x40, matrix products: 126 us -> 151 us  [contract(): lax.dot_general(left_block, right_block, (((0,), (0,)), ((), ())), prefer...]
  transfers between devices with their start and end apart: 3 -> 3, of which waited for: 3 -> 3; matrix products, arithmetic and copies ran while one was open for 0% -> 1% of each run, Pallas kernels for 0% -> 0%
where the time goes in v1:
time: 830 us; the launch traced here: 827 us
  waiting for transfers between devices  371 us (45%)
  matrix products  159 us (19%)
  loops' own time  156 us (19%)
  local copies, waits for them, and re-layouts  121 us (15%)
  between operations  13.9 us (2%)
    all_gather x1, waiting for transfers between devices, body(): gathered = lax.all_gather(factors, 'pair', axis=1, tiled=True)  219 us
    another operation x1, loops' own time, body(): partial_tiles = lax.map(contract, (left_ids, right_ids, weights))  156 us
    dot_general x40, matrix products, contract(): lax.dot_general(left_block, right_block, (((0,), (0,)), ((), ())), prefer...  151 us
    all_gather x1, waiting for transfers between devices, body(): summed = jnp.sum(lax.all_gather(partial_tiles, 'aux'), axis=0)  103 us
    dynamic_slice x120, local copies, waits for them, and re-layouts, body(): partial_tiles = lax.map(contract, (left_ids, right_ids, weights))  70.4 us
    reduce_scatter x1, waiting for transfers between devices, body(): lax.psum_scatter(contribution, 'pair', scatter_dimension=0, tiled=True)  49.3 us
    while x1, local copies, waits for them, and re-layouts, body(): partial_tiles = lax.map(contract, (left_ids, right_ids, weights))  26.9 us
  transfers between devices with their start and end apart: 3, of which 3 were waited for; matrix products, arithmetic and copies ran while one was open for 1% of the time, Pallas kernels for 0%

profile of v1, /device:TPU:0, one launch (start us, length us, event | category | flops | bytes accessed | tf_op | source)
XLA Modules:
  0.0 826.7 jit_solution(7181332357318008237)
XLA Ops:
  7.2 4.4 copy.18
  15.7 218.7 %all-gather.4.cloned.1.call-done = bf16[96,16,64,128]{3,2,0,1:T(8,128)(2,1)} async-done(((bf16[96,2,64,128]{3,2,0,1:T(8,128)(2,1)}), bf16[96,16,64,128]{3,2,0,1:T(8,128)(2,1)}) %all-gather.4.cloned.1.call-update) | async-done | bytes 25165840 | tf_op jit(solution)/shard_map/all_gather | solution.py:29
  234.4 26.9 %copy.19 = bf16[96,16,64,128]{3,0,2,1:T(8,128)(2,1)} copy(bf16[96,16,64,128]{3,2,0,1:T(8,128)(2,1)} %all-gather.4.cloned.1.call-done) | data formatting | bytes 50331648 | tf_op jit(solution)/shard_map/while | solution.py:44
  261.3 376.8 %while.10 = (s32[]{:T(128)}, f32[40,128,128]{2,1,0:T(8,128)}, s32[40]{0:T(128)S(1)}, bf16[96,16,64,128]{3,0,2,1:T(8,128)(2,1)}, s32[40]{0:T(128)S(1)}, /*index=5*/f32[40]{0:T(128)S(1)}, s32[]{:T(128)}, s32[]{:T(128)}, s32[]{:T(128)}) while((s32[]{:T(128)}, f32[40,128,128]{2,1,0:T(8,128)}, s32[40]{0:T(128)S(1)}, ...), condition=%wide.region_4.5_spmd, body=%wide.region_3.4_spmd.sunk | while | flops 201342976 | bytes 3212493 | solution.py:44
  304.5 3.8 fusion.52
  323.4 3.8 fusion.52
  332.8 3.8 fusion.52
  342.2 3.8 fusion.52
  398.8 3.8 fusion.52
  417.6 3.8 fusion.52
  455.3 3.8 fusion.52
  474.1 3.8 fusion.52
  502.4 3.8 fusion.52
  549.5 3.8 fusion.52
  558.9 3.8 fusion.52
  568.4 3.8 fusion.52
  615.4 3.8 fusion.52
  624.9 3.8 fusion.52
  638.4 103.1 %all-gather.6.cloned.1.call-done = f32[160,128,128]{2,1,0:T(8,128)} async-done(((f32[40,128,128]{2,1,0:T(8,128)}), f32[160,128,128]{2,1,0:T(8,128)}) %all-gather.6.cloned.1.call-update) | async-done | bytes 10485776 | tf_op jit(solution)/shard_map/all_gather | solution.py:45
  741.5 5.5 reduce_sum.32
  752.5 4.6 fusion.26
  760.7 4.4 copy.22
  765.1 4.9 reshape.48
  770.9 49.3 %reduce-scatter.2.cloned.1.call-done = f32[2,32,2048]{2,1,0:T(8,128)} async-done(((f32[16,32,2048]{2,1,0:T(8,128)}), f32[2,32,2048]{2,1,0:T(8,128)}) %reduce-scatter.2.cloned.1.call-update) | async-done | bytes 524304 | tf_op jit(solution)/shard_map/reduce_scatter | solution.py:69
  (180 shorter events, 182.6 us)
Async XLA Ops:
  7.2 5.4 copy-start
  7.2 227.2 %all-gather.4.cloned.1.call-start = ((), (), s32[]{:S(2)}) async-start(), calls=%async_computation.1 | async-start | bytes 28311552 | tf_op jit(solution)/shard_map/all_gather | solution.py:29
  11.6 0.7 copy-start.3
  11.6 3.1 copy-start.2
  11.6 729.8 %all-gather.6.cloned.1.call-start = ((), (), s32[]{:S(2)}) async-start(), calls=%async_computation.3 | async-start | bytes 13107200 | tf_op jit(solution)/shard_map/all_gather | solution.py:45
  638.1 182.0 %reduce-scatter.2.cloned.1.call-start = ((), (), s32[]{:S(2)}) async-start(), calls=%async_computation.2 | async-start | bytes 4718592 | tf_op jit(solution)/shard_map/reduce_scatter | solution.py:69
  770.0 50.2 %copy-start.1 = (s32[80,2]{0,1:T(2,128)S(1)}, s32[80,2]{0,1:T(2,128)}, u32[]{:S(2)}) copy-start(s32[80,2]{0,1:T(2,128)} %param.7) | copy-start | bytes 1924
Sparse Core Ops, SparseCore 0:
  11.8 222.5 all-gather.3
  638.2 103.1 all-gather.5
  770.1 50.0 reduce-scatter.1

commit v2 on v0

--- a/solution.py
+++ b/solution.py
@@ -2,6 +2,27 @@
 import jax.numpy as jnp
 from jax import lax
 from jax.sharding import PartitionSpec as P
+
+
+def in_order(blocks, dim):
+    blocks = jnp.moveaxis(blocks, 0, dim)
+    lengths = blocks.shape
+    return blocks.reshape(*lengths[:dim], lengths[dim] * lengths[dim + 1], *lengths[dim + 2 :])
+
+
+def grow_blocks(array, axis):
+    peers, here = (lax.axis_size(axis), lax.axis_index(axis))
+    tiles, distance = (array[None], 1)
+    while distance < peers:
+        other = lax.ppermute(tiles, axis, [(i, i ^ distance) for i in range(peers)])
+        low = here & distance == 0
+        tiles = jnp.concatenate([jnp.where(low, tiles, other), jnp.where(low, other, tiles)])
+        distance *= 2
+    return tiles
+
+
+def gather_by_bits(value, axis, dim):
+    return in_order(grow_blocks(value, axis), dim)
 
 
 def body(factors, pairs, shared, owners):
@@ -26,7 +47,7 @@
     left_ids = pairs[picked, 0]
     right_ids = pairs[picked, 1]
     weights = live_slot * shared[picked, 0].astype(jnp.float32)
-    gathered = lax.all_gather(factors, "pair", axis=1, tiled=True)
+    gathered = gather_by_bits(factors, "pair", 1)
 
     def contract(slot_item):
         left_id, right_id, slot_scale = slot_item

time: 891 us -> 1410 us (1.58)
  waiting for transfers between devices: 344 us -> 807 us
  other arithmetic: 0.45 us -> 56.2 us
    ppermute x0 -> x3, waiting for transfers between devices: none -> 678 us  [grow_blocks(): other = lax.ppermute(tiles, axis, [(i, i ^ distance) for i in range(peers)])]
    all_gather x1 -> x0, waiting for transfers between devices: 219 us -> none  [body(): gathered = lax.all_gather(factors, 'pair', axis=1, tiled=True)]
    transpose x0 -> x1, local copies, waits for them, and re-layouts: none -> 26.9 us  [in_order(): blocks = jnp.moveaxis(blocks, 0, dim)]
    while x1 -> x0, local copies, waits for them, and re-layouts: 26.9 us -> none  [body(): partial_tiles = lax.map(contract, (left_ids, right_ids, weights))]
    select_n x0 -> x3, other arithmetic: none -> 24.8 us  [grow_blocks(): jnp.where(low, tiles, other)]
    transpose x0 -> x1, other arithmetic: none -> 20.5 us  [in_order(): blocks = jnp.moveaxis(blocks, 0, dim)]
  transfers between devices with their start and end apart: 3 -> 5, of which waited for: 3 -> 5; matrix products, arithmetic and copies ran while one was open for 0% -> 0% of each run, Pallas kernels for 0% -> 0%
where the time goes in v2:
time: 1410 us
  waiting for transfers between devices  807 us (57%)
  local copies, waits for them, and re-layouts  235 us (17%)
  loops' own time  156 us (11%)
  matrix products  133 us (9%)
  other arithmetic  56.2 us (4%)
  between operations  14.2 us (1%)
    ppermute x3, waiting for transfers between devices, grow_blocks(): other = lax.ppermute(tiles, axis, [(i, i ^ distance) for i in range(peers)])  678 us
    another operation x1, loops' own time, body(): partial_tiles = lax.map(contract, (left_ids, right_ids, weights))  156 us
    dot_general x40, matrix products, contract(): lax.dot_general(left_block, right_block, (((0,), (0,)), ((), ())), prefer...  126 us
    dynamic_update_slice x40, local copies, waits for them, and re-layouts, body(): partial_tiles = lax.map(contract, (left_ids, right_ids, weights))  118 us
    psum x1, waiting for transfers between devices, body(): summed = lax.psum(partial_tiles, 'aux')  79.2 us
    dynamic_slice x120, local copies, waits for them, and re-layouts, body(): partial_tiles = lax.map(contract, (left_ids, right_ids, weights))  70.4 us
    reduce_scatter x1, waiting for transfers between devices, body(): lax.psum_scatter(contribution, 'pair', scatter_dimension=0, tiled=True)  49.2 us
  transfers between devices with their start and end apart: 5, of which 5 were waited for; matrix products, arithmetic and copies ran while one was open for 0% of the time, Pallas kernels for 0%

profile of v2, /device:TPU:0, one launch (start us, length us, event | category | flops | bytes accessed | tf_op | source)
XLA Modules:
  0.0 1407.2 jit_solution(1579510717877265110)
XLA Ops:
  7.7 5.6 collective-permute-done
  13.4 3.3 broadcast_select_fusion.5
  16.6 3.5 pad_maximum_fusion.1
  23.1 136.1 %collective-permute-done.1 = bf16[2,96,2,64,128]{4,3,2,1,0:T(8,128)(2,1)} collective-permute-done((bf16[2,96,2,64,128]{4,3,2,1,0:T(8,128)(2,1)}, bf16[2,96,2,64,128]{4,3,2,1,0:T(8,128)(2,1)}, u32[]{:S(2)}, u32[]{:S(2)}) %collective-permute-start.1) | collective-permute-done | bytes 6291488 | tf_op jit(solution)/shard_map/ppermute | solution.py:17
  159.2 4.7 broadcast_select_fusion.3
  164.0 6.9 pad_maximum_fusion
  178.4 536.5 %collective-permute-done.2 = bf16[4,96,2,64,128]{4,3,2,1,0:T(8,128)(2,1)} collective-permute-done((bf16[4,96,2,64,128]{4,3,2,1,0:T(8,128)(2,1)}, bf16[4,96,2,64,128]{4,3,2,1,0:T(8,128)(2,1)}, u32[]{:S(2)}, u32[]{:S(2)}) %collective-permute-start.2) | collective-permute-done | bytes 12582944 | tf_op jit(solution)/shard_map/ppermute | solution.py:17
  715.0 16.9 %broadcast_select_fusion.1 = (bf16[4,96,2,64,128]{4,3,2,1,0:T(8,128)(2,1)}, bf16[4,96,2,64,128]{4,3,2,1,0:T(8,128)(2,1)}) fusion(bf16[4,96,2,64,128]{4,3,2,1,0:T(8,128)(2,1)} %collective-permute-done.2, pred[]{:T(512)S(6)} %eq.82, bf16[2,96,2,64,128]{4,3,2,1,0:T(8,128)(2,1)} %copy-done.4, bf16[2,96,2,64,128]{4,3,2,1,0:T(8,128)(2,1)} %copy-done.3), kind=kLoop, calls=%fused_computation.14 | loop fusion | flops 18874368 | bytes 50331648 | tf_op jit(solution)/shard_map/jit(_where)/select_n | solution.py:19
  731.8 20.5 %maximum_bitcast_fusion = bf16[96,8,2,64,128]{4,3,2,0,1:T(8,128)(2,1)} fusion(bf16[4,96,2,64,128]{4,3,2,1,0:T(8,128)(2,1)} %get-tuple-element.48, bf16[4,96,2,64,128]{4,3,2,1,0:T(8,128)(2,1)} %get-tuple-element.47), kind=kLoop, calls=%fused_computation.11 | loop fusion | flops 12582912 | bytes 50331648 | tf_op jit(solution)/shard_map/transpose | solution.py:8
  752.4 26.9 %copy.14 = bf16[96,8,2,64,128]{4,0,3,2,1:T(8,128)(2,1)} copy(bf16[96,8,2,64,128]{4,3,2,0,1:T(8,128)(2,1)} %maximum_bitcast_fusion) | data formatting | bytes 50331648 | tf_op jit(solution)/shard_map/transpose | solution.py:8
  779.2 470.2 %while.10 = (s32[]{:T(128)}, f32[40,128,128]{2,0,1:T(8,128)}, s32[40]{0:T(128)S(1)}, bf16[96,16,64,128]{3,0,2,1:T(8,128)(2,1)}, s32[40]{0:T(128)S(1)}, /*index=5*/f32[40]{0:T(128)S(1)}, s32[]{:T(128)}, s32[]{:T(128)}, s32[]{:T(128)}) while((s32[]{:T(128)}, f32[40,128,128]{2,0,1:T(8,128)}, s32[40]{0:T(128)S(1)}, ...), condition=%wide.region_4.5_spmd, body=%wide.region_3.4_spmd.sunk | while | flops 201342976 | bytes 3343057 | solution.py:65
  796.6 3.1 fusion.42
  820.1 3.1 fusion.42
  878.8 3.2 fusion.42
  1008.2 3.2 fusion.42
  1043.5 3.2 fusion.42
  1196.4 3.1 fusion.42
  1219.9 3.1 fusion.42
  1249.8 79.2 %all-reduce.4.cloned.1.call-done = f32[40,128,128]{2,0,1:T(8,128)} async-done(((f32[40,128,128]{2,0,1:T(8,128)}), f32[40,128,128]{2,0,1:T(8,128)}) %all-reduce.4.cloned.1.call-update) | async-done | bytes 2621456 | tf_op jit(solution)/shard_map/psum | solution.py:66
  1333.8 3.4 fusion.17
  1337.2 3.6 add_bitcast_fusion
  1340.8 4.4 copy.17
  1345.2 4.9 reshape.52
  1351.1 49.2 %reduce-scatter.2.cloned.1.call-done = f32[2,32,2048]{2,1,0:T(8,128)} async-done(((f32[16,32,2048]{2,1,0:T(8,128)}), f32[2,32,2048]{2,1,0:T(8,128)}) %reduce-scatter.2.cloned.1.call-update) | async-done | bytes 524304 | tf_op jit(solution)/shard_map/reduce_scatter | solution.py:90
  (233 shorter events, 309.5 us)
Async XLA Ops:
  7.2 168.2 %copy-start = (s32[80,2]{0,1:T(2,128)S(1)}, s32[80,2]{0,1:T(2,128)}, u32[]{:S(2)}) copy-start(s32[80,2]{0,1:T(2,128)} %param.7) | copy-start | bytes 1924
  7.2 1321.8 %all-reduce.4.cloned.1.call-start = ((), (), s32[]{:S(2)}) async-start(), calls=%async_computation.1 | async-start | bytes 5242880 | tf_op jit(solution)/shard_map/psum | solution.py:66
  7.2 6.1 collective-permute-start
  16.6 3.5 copy-start.5
  20.2 139.1 %collective-permute-start.1 = (bf16[2,96,2,64,128]{4,3,2,1,0:T(8,128)(2,1)}, bf16[2,96,2,64,128]{4,3,2,1,0:T(8,128)(2,1)}, u32[]{:S(2)}, u32[]{:S(2)}) collective-permute-start(bf16[2,96,2,64,128]{4,3,2,1,0:T(8,128)(2,1)} %pad_maximum_fusion.1), channel_id=1, source_target_pairs={{0,8},{4,12},{8,0},{12,4},{16,24},{20,28},{24,16},{28,20},{1,9},{5... | collective-permute-start | bytes 18874376 | tf_op jit(solution)/shard_map/ppermute | solution.py:17
  163.9 7.0 copy-start.3
  163.9 8.3 copy-start.4
  163.9 11.1 copy-start.6
  164.0 13.5 copy-start.2
  172.2 542.7 %collective-permute-start.2 = (bf16[4,96,2,64,128]{4,3,2,1,0:T(8,128)(2,1)}, bf16[4,96,2,64,128]{4,3,2,1,0:T(8,128)(2,1)}, u32[]{:S(2)}, u32[]{:S(2)}) collective-permute-start(bf16[4,96,2,64,128]{4,3,2,1,0:T(8,128)(2,1)} %pad_maximum_fusion), channel_id=1, source_target_pairs={{0,16},{4,20},{8,24},{12,28},{16,0},{20,4},{24,8},{28,12},{1,17},{... | collective-permute-start | bytes 37748744 | tf_op jit(solution)/shard_map/ppermute | solution.py:17
  1249.5 150.8 %reduce-scatter.2.cloned.1.call-start = ((), (), s32[]{:S(2)}) async-start(), calls=%async_computation.2 | async-start | bytes 4718592 | tf_op jit(solution)/shard_map/reduce_scatter | solution.py:90
  1340.8 59.5 %copy-start.1 = (s32[80,2]{0,1:T(2,128)S(1)}, s32[80,2]{0,1:T(2,128)}, u32[]{:S(2)}) copy-start(s32[80,2]{0,1:T(2,128)} %param.7) | copy-start | bytes 1924
Sparse Core Ops, SparseCore 0:
  1249.6 79.3 all-reduce.3
  1350.3 49.9 reduce-scatter.1
